TPU v7x, 512 devices: a whole 4x4x16 slice. The times are simulated.
512 devices in a mesh: rx: 8 (over z_hi, y), ry: 8 (over z_lo), tp: 8 (over x, core).
Axes of the slice: x: 4, y: 4, z: 16 (z_hi: 2, z_lo: 8; z = z_hi * 8 + z_lo), core: 2. Of those that a mesh axis runs over, the one named last changes fastest.
Arguments:
- weight: float32 [8, 8, 192, 4096], P('rx', 'ry', 'tp'), may hold values from -6 to 6
- public: float32 [8, 8, 192, 4096], P('rx', 'ry', 'tp'), may hold values from -6 to 6
- mixture: float32 [8, 8, 192, 4096], P('rx', 'ry', 'tp'), may hold values from -6 to 6
- moment_one: float32 [8, 8, 192, 4096], P('rx', 'ry', 'tp'), may hold values from -0.6 to 0.6
- moment_two: float32 [8, 8, 192, 4096], P('rx', 'ry', 'tp'), may hold values from 0.01 to 1
- stored: bfloat16 [8, 8, 192, 1024], P('rx', 'ry', 'tp'), may hold values from -6 to 6
- out_grad: bfloat16 [8, 8, 1024, 4096], P('rx', 'ry', 'tp'), may hold values from -0.5 to 0.5
Outputs:
- weight_new: float32 [8, 8, 192, 4096], P('rx', 'ry', 'tp')
- public_new: float32 [8, 8, 192, 4096], P('rx', 'ry', 'tp')
- mixture_new: float32 [8, 8, 192, 4096], P('rx', 'ry', 'tp')
- first_new: float32 [8, 8, 192, 4096], P('rx', 'ry', 'tp')
- second_new: float32 [8, 8, 192, 4096], P('rx', 'ry', 'tp')
All inputs are finite; a program needn't handle non-finite values.
Results may differ from a plain program's by a relative error of at most 0.0039.
Values may be sent and summed in bfloat16 or wider, within the bound.
A program may use at most 64 MiB of HBM per device.

v0:
```python
import jax
import jax.numpy as jnp
from jax import lax
from jax.sharding import PartitionSpec as P

ROUNDS = 2


beta_one = 0.9
beta_two = 0.95
first_fix = 0.9999734386011124
second_fix = 0.994079470779666
learn_rate = 0.02
decay_rate = 0.1
epsilon = 1e-08
step_size = 0.5


def cut_along(shard, dim, devices):
    shape = shard.shape
    parts = shard.reshape(*shape[:dim], devices, shape[dim] // devices, *shape[dim + 1 :])
    return jnp.moveaxis(parts, dim, 0)


def sum_at_owner(shard, axis, dim):
    devices = lax.axis_size(axis)
    parts = lax.all_to_all(cut_along(shard, dim, devices), axis, 0, 0, tiled=True)
    return jnp.sum(parts.astype(jnp.float32), axis=0)


def with_halo(shard, sides, width):
    edges = {}
    for axis, dim in sides:
        devices, length = (lax.axis_size(axis), shard.shape[dim])
        up = [(i, (i + 1) % devices) for i in range(devices)]
        last = lax.slice_in_dim(shard, length - width, length, axis=dim)
        initial = lax.slice_in_dim(shard, 0, width, axis=dim)
        edges[dim] = (
            lax.ppermute(last, axis, up),
            lax.ppermute(initial, axis, [(b, a) for a, b in up]),
        )
    done = []
    for _, dim in sides:
        low, high = edges[dim]
        around = [(width, width) if d in done else (0, 0) for d in range(shard.ndim)]
        shard = jnp.concatenate([jnp.pad(low, around), shard, jnp.pad(high, around)], axis=dim)
        done.append(dim)
    return shard


def per_device(weight, public, mixture, moment_one, moment_two, stored, out_grad):
    local_acts = stored[0, 0]
    local_grad = out_grad[0, 0]
    gathered = lax.all_to_all(local_acts, "tp", split_axis=1, concat_axis=0, tiled=True)
    all_terms = jnp.dot(gathered, local_grad, preferred_element_type=jnp.float32)
    gradient = sum_at_owner(all_terms.astype(jnp.bfloat16), "tp", 0)
    gradient = gradient[None, None]
    first_new = beta_one * moment_one + (1.0 - beta_one) * gradient
    second_new = beta_two * moment_two + (1.0 - beta_two) * gradient * gradient
    adjusted = first_new / first_fix / (jnp.sqrt(second_new / second_fix) + epsilon)
    current = weight - learn_rate * (adjusted + decay_rate * weight)
    public_new = public
    mixture_new = mixture
    for gossip_turn in range(ROUNDS):
        sent = (current - public_new).astype(jnp.bfloat16)
        framed = with_halo(sent, (("rx", 0), ("ry", 1)), 1)
        beside_all = (
            framed[0:1, 1:2].astype(jnp.float32)
            + framed[2:3, 1:2].astype(jnp.float32)
            + framed[1:2, 0:1].astype(jnp.float32)
            + framed[1:2, 2:3].astype(jnp.float32)
        )
        own_sent = sent.astype(jnp.float32)
        public_new = public_new + own_sent
        mixture_new = mixture_new + (own_sent + beside_all) / 5.0
        current = current + step_size * (mixture_new - public_new)
    return (current, public_new, mixture_new, first_new, second_new)


def solution(mesh):
    in_specs = (
        P("rx", "ry", "tp", None),
        P("rx", "ry", "tp", None),
        P("rx", "ry", "tp", None),
        P("rx", "ry", "tp", None),
        P("rx", "ry", "tp", None),
        P("rx", "ry", "tp", None),
        P("rx", "ry", "tp", None),
    )
    out_specs = (
        P("rx", "ry", "tp", None),
        P("rx", "ry", "tp", None),
        P("rx", "ry", "tp", None),
        P("rx", "ry", "tp", None),
        P("rx", "ry", "tp", None),
    )
    return jax.shard_map(
        per_device, mesh=mesh, in_specs=in_specs, out_specs=out_specs, check_vma=False
    )
```

profile of v0, /device:TPU:1, one launch (start us, length us, event | category | flops | bytes accessed | tf_op | source)
XLA Modules:
  0.0 130.7 jit_solution(9283960108540173803)
XLA Ops:
  0.6 0.0 copy-start
  0.6 0.9 copy.14
  1.6 14.0 %all_to_all.24 = bf16[24,8,128]{2,0,1:T(8,128)(2,1)S(1)} all-to-all(bf16[24,8,128]{2,0,1:T(8,128)(2,1)S(1)} %copy.13), channel_id=1, replica_groups=mesh['rx'=8,'ry'=8,'tp'=8] {'tp'}, dimensions={1} | all-to-all | bytes 98304 | tf_op jit(solution)/shard_map/all_to_all | solution.py:54
  15.5 0.0 copy-done
  15.5 0.6 convolution_convert_fusion
  16.1 23.7 %all_to_all.25 = bf16[8,24,4096]{2,1,0:T(8,128)(2,1)S(1)} all-to-all(bf16[8,24,4096]{2,1,0:T(8,128)(2,1)S(1)} %bitcast.19), channel_id=1, replica_groups=mesh['rx'=8,'ry'=8,'tp'=8] {'tp'}, dimensions={0} | all-to-all | bytes 3145728 | tf_op jit(solution)/shard_map/all_to_all | solution.py:27
  39.8 0.0 copy-start.1
  39.9 0.0 copy-start.3
  39.9 0.0 copy-start.4
  39.9 0.0 copy-start.5
  39.9 0.2 convert_reduce_fusion
  40.1 0.8 copy-done.1
  40.8 0.1 copy-done.3
  41.0 0.1 copy-done.4
  41.1 0.1 copy-done.5
  41.2 0.0 copy-start.2
  41.2 1.2 subtract_convert_fusion.1
  42.4 9.2 %collective-permute-start.3 = (bf16[1,1,24,4096]{3,2,1,0:T(8,128)(2,1)S(1)}, bf16[1,1,24,4096]{3,2,1,0:T(8,128)(2,1)S(1)}, u32[]{:S(2)}, u32[]{:S(2)}) collective-permute-start(bf16[1,1,24,4096]{3,2,1,0:T(8,128)(2,1)S(1)} %get-tuple-element.8), channel_id=1, source_target_pairs={{8,0},{16,8},{24,16},{32,24},{40,32},{48,40},{56,48},{0,56},{9,1},... | collective-permute-start | bytes 589832 | tf_op jit(solution)/shard_map/ppermute | solution.py:40
  51.6 1.9 %collective-permute-start.2 = (bf16[1,1,24,4096]{3,2,1,0:T(8,128)(2,1)S(1)}, bf16[1,1,24,4096]{3,2,1,0:T(8,128)(2,1)S(1)}, u32[]{:S(2)}, u32[]{:S(2)}) collective-permute-start(bf16[1,1,24,4096]{3,2,1,0:T(8,128)(2,1)S(1)} %get-tuple-element.8), channel_id=1, source_target_pairs={{0,8},{8,16},{16,24},{24,32},{32,40},{40,48},{48,56},{56,0},{1,9},... | collective-permute-start | bytes 589832 | tf_op jit(solution)/shard_map/ppermute | solution.py:39
  53.6 10.4 %collective-permute-start.1 = (bf16[1,1,24,4096]{3,2,1,0:T(8,128)(2,1)S(1)}, bf16[1,1,24,4096]{3,2,1,0:T(8,128)(2,1)S(1)}, u32[]{:S(2)}, u32[]{:S(2)}) collective-permute-start(bf16[1,1,24,4096]{3,2,1,0:T(8,128)(2,1)S(1)} %get-tuple-element.8), channel_id=1, source_target_pairs={{64,0},{128,64},{192,128},{256,192},{320,256},{384,320},{448,384},... | collective-permute-start | bytes 589832 | tf_op jit(solution)/shard_map/ppermute | solution.py:40
  64.0 1.9 %collective-permute-start = (bf16[1,1,24,4096]{3,2,1,0:T(8,128)(2,1)S(1)}, bf16[1,1,24,4096]{3,2,1,0:T(8,128)(2,1)S(1)}, u32[]{:S(2)}, u32[]{:S(2)}) collective-permute-start(bf16[1,1,24,4096]{3,2,1,0:T(8,128)(2,1)S(1)} %get-tuple-element.8), channel_id=1, source_target_pairs={{0,64},{64,128},{128,192},{192,256},{256,320},{320,384},{384,448},... | collective-permute-start | bytes 589832 | tf_op jit(solution)/shard_map/ppermute | solution.py:39
  65.9 0.0 collective-permute-done.3
  65.9 7.1 %collective-permute-done.2 = bf16[1,1,24,4096]{3,2,1,0:T(8,128)(2,1)S(1)} collective-permute-done((bf16[1,1,24,4096]{3,2,1,0:T(8,128)(2,1)S(1)}, bf16[1,1,24,4096]{3,2,1,0:T(8,128)(2,1)S(1)}, u32[]{:S(2)}, u32[]{:S(2)}) %collective-permute-start.2) | collective-permute-done | bytes 196640 | tf_op jit(solution)/shard_map/ppermute | solution.py:39
  73.1 6.1 %collective-permute-done.1 = bf16[1,1,24,4096]{3,2,1,0:T(8,128)(2,1)S(1)} collective-permute-done((bf16[1,1,24,4096]{3,2,1,0:T(8,128)(2,1)S(1)}, bf16[1,1,24,4096]{3,2,1,0:T(8,128)(2,1)S(1)}, u32[]{:S(2)}, u32[]{:S(2)}) %collective-permute-start.1) | collective-permute-done | bytes 196640 | tf_op jit(solution)/shard_map/ppermute | solution.py:40
  79.2 12.4 %collective-permute-done = bf16[1,1,24,4096]{3,2,1,0:T(8,128)(2,1)S(1)} collective-permute-done((bf16[1,1,24,4096]{3,2,1,0:T(8,128)(2,1)S(1)}, bf16[1,1,24,4096]{3,2,1,0:T(8,128)(2,1)S(1)}, u32[]{:S(2)}, u32[]{:S(2)}) %collective-permute-start) | collective-permute-done | bytes 196640 | tf_op jit(solution)/shard_map/ppermute | solution.py:39
  91.6 0.0 copy-done.2
  91.6 0.2 subtract_convert_fusion
  91.8 6.4 %collective-permute-start.7 = (bf16[1,1,24,4096]{3,2,1,0:T(8,128)(2,1)S(1)}, bf16[1,1,24,4096]{3,2,1,0:T(8,128)(2,1)S(1)}, u32[]{:S(2)}, u32[]{:S(2)}) collective-permute-start(bf16[1,1,24,4096]{3,2,1,0:T(8,128)(2,1)S(1)} %subtract_convert_fusion), channel_id=1, source_target_pairs={{8,0},{16,8},{24,16},{32,24},{40,32},{48,40},{56,48},{0,56},{9,1},... | collective-permute-start | bytes 589832 | tf_op jit(solution)/shard_map/ppermute | solution.py:40
  98.3 1.9 %collective-permute-start.6 = (bf16[1,1,24,4096]{3,2,1,0:T(8,128)(2,1)S(1)}, bf16[1,1,24,4096]{3,2,1,0:T(8,128)(2,1)S(1)}, u32[]{:S(2)}, u32[]{:S(2)}) collective-permute-start(bf16[1,1,24,4096]{3,2,1,0:T(8,128)(2,1)S(1)} %subtract_convert_fusion), channel_id=1, source_target_pairs={{0,8},{8,16},{16,24},{24,32},{32,40},{40,48},{48,56},{56,0},{1,9},... | collective-permute-start | bytes 589832 | tf_op jit(solution)/shard_map/ppermute | solution.py:39
  100.2 1.9 %collective-permute-start.5 = (bf16[1,1,24,4096]{3,2,1,0:T(8,128)(2,1)S(1)}, bf16[1,1,24,4096]{3,2,1,0:T(8,128)(2,1)S(1)}, u32[]{:S(2)}, u32[]{:S(2)}) collective-permute-start(bf16[1,1,24,4096]{3,2,1,0:T(8,128)(2,1)S(1)} %subtract_convert_fusion), channel_id=1, source_target_pairs={{64,0},{128,64},{192,128},{256,192},{320,256},{384,320},{448,384},... | collective-permute-start | bytes 589832 | tf_op jit(solution)/shard_map/ppermute | solution.py:40
  102.2 3.4 %collective-permute-start.4 = (bf16[1,1,24,4096]{3,2,1,0:T(8,128)(2,1)S(1)}, bf16[1,1,24,4096]{3,2,1,0:T(8,128)(2,1)S(1)}, u32[]{:S(2)}, u32[]{:S(2)}) collective-permute-start(bf16[1,1,24,4096]{3,2,1,0:T(8,128)(2,1)S(1)} %subtract_convert_fusion), channel_id=1, source_target_pairs={{0,64},{64,128},{128,192},{192,256},{256,320},{320,384},{384,448},... | collective-permute-start | bytes 589832 | tf_op jit(solution)/shard_map/ppermute | solution.py:39
  105.5 5.7 %collective-permute-done.7 = bf16[1,1,24,4096]{3,2,1,0:T(8,128)(2,1)S(1)} collective-permute-done((bf16[1,1,24,4096]{3,2,1,0:T(8,128)(2,1)S(1)}, bf16[1,1,24,4096]{3,2,1,0:T(8,128)(2,1)S(1)}, u32[]{:S(2)}, u32[]{:S(2)}) %collective-permute-start.7) | collective-permute-done | bytes 196640 | tf_op jit(solution)/shard_map/ppermute | solution.py:40
  111.2 7.8 %collective-permute-done.6 = bf16[1,1,24,4096]{3,2,1,0:T(8,128)(2,1)S(1)} collective-permute-done((bf16[1,1,24,4096]{3,2,1,0:T(8,128)(2,1)S(1)}, bf16[1,1,24,4096]{3,2,1,0:T(8,128)(2,1)S(1)}, u32[]{:S(2)}, u32[]{:S(2)}) %collective-permute-start.6) | collective-permute-done | bytes 196640 | tf_op jit(solution)/shard_map/ppermute | solution.py:39
  119.0 4.8 %collective-permute-done.5 = bf16[1,1,24,4096]{3,2,1,0:T(8,128)(2,1)S(1)} collective-permute-done((bf16[1,1,24,4096]{3,2,1,0:T(8,128)(2,1)S(1)}, bf16[1,1,24,4096]{3,2,1,0:T(8,128)(2,1)S(1)}, u32[]{:S(2)}, u32[]{:S(2)}) %collective-permute-start.5) | collective-permute-done | bytes 196640 | tf_op jit(solution)/shard_map/ppermute | solution.py:40
  123.9 5.4 %collective-permute-done.4 = bf16[1,1,24,4096]{3,2,1,0:T(8,128)(2,1)S(1)} collective-permute-done((bf16[1,1,24,4096]{3,2,1,0:T(8,128)(2,1)S(1)}, bf16[1,1,24,4096]{3,2,1,0:T(8,128)(2,1)S(1)}, u32[]{:S(2)}, u32[]{:S(2)}) %collective-permute-start.4) | collective-permute-done | bytes 196640 | tf_op jit(solution)/shard_map/ppermute | solution.py:39
  129.3 1.4 %multiply_add_fusion = (f32[1,1,24,4096]{3,2,1,0:T(8,128)}, f32[1,1,24,4096]{3,2,1,0:T(8,128)}, f32[1,1,24,4096]{3,2,1,0:T(8,128)}) fusion(f32[1,1,24,4096]{3,2,1,0:T(8,128)S(1)} %get-tuple-element.9, f32[1,1,24,4096]{3,2,1,0:T(8,128)S(1)} %copy-done.1, bf16[1,1,24,4096]{3,2,1,0:T(8,128)(2,1)S(1)} %get-tuple-element.8, f32[1,1,24,4096]{3,2,1,0:T(8,128)S(1)} %copy-done.2, ...), kind=kLoop, calls=%fused_computation.15 | loop fusion | flops 2949120 | bytes 4325376 | tf_op jit(solution)/shard_map/add | solution.py:76
  (1 shorter events, 0.0 us)
Async XLA Ops:
  0.6 14.9 %copy-start = (bf16[1,1,128,4096]{3,2,1,0:T(8,128)(2,1)S(1)}, bf16[1,1,128,4096]{3,2,1,0:T(8,128)(2,1)}, u32[]{:S(2)}) copy-start(bf16[1,1,128,4096]{3,2,1,0:T(8,128)(2,1)} %param.13) | copy-start | bytes 3145732
  39.8 1.0 copy-start.1
  39.9 1.1 copy-start.3
  39.9 1.2 copy-start.4
  39.9 1.3 %copy-start.5 = (f32[1,1,24,4096]{3,2,1,0:T(8,128)S(1)}, f32[1,1,24,4096]{3,2,1,0:T(8,128)}, u32[]{:S(2)}) copy-start(f32[1,1,24,4096]{3,2,1,0:T(8,128)} %param.11) | copy-start | bytes 1179652
  41.2 50.4 %copy-start.2 = (f32[1,1,24,4096]{3,2,1,0:T(8,128)S(1)}, f32[1,1,24,4096]{3,2,1,0:T(8,128)}, u32[]{:S(2)}) copy-start(f32[1,1,24,4096]{3,2,1,0:T(8,128)} %param.9) | copy-start | bytes 1179652
  42.4 23.5 %collective-permute-start.3 = (bf16[1,1,24,4096]{3,2,1,0:T(8,128)(2,1)S(1)}, bf16[1,1,24,4096]{3,2,1,0:T(8,128)(2,1)S(1)}, u32[]{:S(2)}, u32[]{:S(2)}) collective-permute-start(bf16[1,1,24,4096]{3,2,1,0:T(8,128)(2,1)S(1)} %get-tuple-element.8), channel_id=1, source_target_pairs={{8,0},{16,8},{24,16},{32,24},{40,32},{48,40},{56,48},{0,56},{9,1},... | collective-permute-start | bytes 589832 | tf_op jit(solution)/shard_map/ppermute | solution.py:40
  51.6 21.4 %collective-permute-start.2 = (bf16[1,1,24,4096]{3,2,1,0:T(8,128)(2,1)S(1)}, bf16[1,1,24,4096]{3,2,1,0:T(8,128)(2,1)S(1)}, u32[]{:S(2)}, u32[]{:S(2)}) collective-permute-start(bf16[1,1,24,4096]{3,2,1,0:T(8,128)(2,1)S(1)} %get-tuple-element.8), channel_id=1, source_target_pairs={{0,8},{8,16},{16,24},{24,32},{32,40},{40,48},{48,56},{56,0},{1,9},... | collective-permute-start | bytes 589832 | tf_op jit(solution)/shard_map/ppermute | solution.py:39
  53.6 25.6 %collective-permute-start.1 = (bf16[1,1,24,4096]{3,2,1,0:T(8,128)(2,1)S(1)}, bf16[1,1,24,4096]{3,2,1,0:T(8,128)(2,1)S(1)}, u32[]{:S(2)}, u32[]{:S(2)}) collective-permute-start(bf16[1,1,24,4096]{3,2,1,0:T(8,128)(2,1)S(1)} %get-tuple-element.8), channel_id=1, source_target_pairs={{64,0},{128,64},{192,128},{256,192},{320,256},{384,320},{448,384},... | collective-permute-start | bytes 589832 | tf_op jit(solution)/shard_map/ppermute | solution.py:40
  64.0 27.7 %collective-permute-start = (bf16[1,1,24,4096]{3,2,1,0:T(8,128)(2,1)S(1)}, bf16[1,1,24,4096]{3,2,1,0:T(8,128)(2,1)S(1)}, u32[]{:S(2)}, u32[]{:S(2)}) collective-permute-start(bf16[1,1,24,4096]{3,2,1,0:T(8,128)(2,1)S(1)} %get-tuple-element.8), channel_id=1, source_target_pairs={{0,64},{64,128},{128,192},{192,256},{256,320},{320,384},{384,448},... | collective-permute-start | bytes 589832 | tf_op jit(solution)/shard_map/ppermute | solution.py:39
  91.8 19.4 %collective-permute-start.7 = (bf16[1,1,24,4096]{3,2,1,0:T(8,128)(2,1)S(1)}, bf16[1,1,24,4096]{3,2,1,0:T(8,128)(2,1)S(1)}, u32[]{:S(2)}, u32[]{:S(2)}) collective-permute-start(bf16[1,1,24,4096]{3,2,1,0:T(8,128)(2,1)S(1)} %subtract_convert_fusion), channel_id=1, source_target_pairs={{8,0},{16,8},{24,16},{32,24},{40,32},{48,40},{56,48},{0,56},{9,1},... | collective-permute-start | bytes 589832 | tf_op jit(solution)/shard_map/ppermute | solution.py:40
  98.3 20.7 %collective-permute-start.6 = (bf16[1,1,24,4096]{3,2,1,0:T(8,128)(2,1)S(1)}, bf16[1,1,24,4096]{3,2,1,0:T(8,128)(2,1)S(1)}, u32[]{:S(2)}, u32[]{:S(2)}) collective-permute-start(bf16[1,1,24,4096]{3,2,1,0:T(8,128)(2,1)S(1)} %subtract_convert_fusion), channel_id=1, source_target_pairs={{0,8},{8,16},{16,24},{24,32},{32,40},{40,48},{48,56},{56,0},{1,9},... | collective-permute-start | bytes 589832 | tf_op jit(solution)/shard_map/ppermute | solution.py:39
  100.2 23.7 %collective-permute-start.5 = (bf16[1,1,24,4096]{3,2,1,0:T(8,128)(2,1)S(1)}, bf16[1,1,24,4096]{3,2,1,0:T(8,128)(2,1)S(1)}, u32[]{:S(2)}, u32[]{:S(2)}) collective-permute-start(bf16[1,1,24,4096]{3,2,1,0:T(8,128)(2,1)S(1)} %subtract_convert_fusion), channel_id=1, source_target_pairs={{64,0},{128,64},{192,128},{256,192},{320,256},{384,320},{448,384},... | collective-permute-start | bytes 589832 | tf_op jit(solution)/shard_map/ppermute | solution.py:40
  102.2 27.1 %collective-permute-start.4 = (bf16[1,1,24,4096]{3,2,1,0:T(8,128)(2,1)S(1)}, bf16[1,1,24,4096]{3,2,1,0:T(8,128)(2,1)S(1)}, u32[]{:S(2)}, u32[]{:S(2)}) collective-permute-start(bf16[1,1,24,4096]{3,2,1,0:T(8,128)(2,1)S(1)} %subtract_convert_fusion), channel_id=1, source_target_pairs={{0,64},{64,128},{128,192},{192,256},{256,320},{320,384},{384,448},... | collective-permute-start | bytes 589832 | tf_op jit(solution)/shard_map/ppermute | solution.py:39
where the time goes:
time: 131 us
  waiting for transfers between devices  49.5 us (38%)
  blocking collectives  37.7 us (29%)
  starting transfers between devices  37.1 us (28%)
  other arithmetic  2.97 us (2%)
  local copies, waits for them, and re-layouts  2.05 us (2%)
    ppermute x4, waiting for transfers between devices, with_halo(): lax.ppermute(last, axis, up)  32.8 us
    ppermute x4, starting transfers between devices, with_halo(): lax.ppermute(initial, axis, [(b, a) for a, b in up])  28 us
    all_to_all x1, blocking collectives, sum_at_owner(): lax.all_to_all(cut_along(shard, dim, devices), axis, 0, 0, tiled=True)  23.7 us
    ppermute x4, waiting for transfers between devices, with_halo(): lax.ppermute(initial, axis, [(b, a) for a, b in up])  16.7 us
    all_to_all x1, blocking collectives, per_device(): lax.all_to_all(local_acts, 'tp', split_axis=1, concat_axis=0, tiled=True)  14 us
    ppermute x4, starting transfers between devices, with_halo(): lax.ppermute(last, axis, up)  9.12 us
  transfers between devices with their start and end apart: 8, of which 7 were waited for; matrix products, arithmetic and copies ran while one was open for 0% of the time, Pallas kernels for 0%

commit v1 on v0

v1 whole, which is shorter than its diff:
```python
import functools

import jax
import jax.numpy as jnp
from jax import lax
from jax.experimental import pallas as pl
from jax.experimental.pallas import tpu as pltpu
from jax.sharding import PartitionSpec as P

MESH = pl.DeviceIdType.MESH
ROUNDS = 2
CHUNKS = 4

beta_one = 0.9
beta_two = 0.95
first_fix = 0.9999734386011124
second_fix = 0.994079470779666
learn_rate = 0.02
decay_rate = 0.1
epsilon = 1e-08
step_size = 0.5


def kernel(
    weight_in, public_in, mixture_in, one_in, two_in, stored_in, grad_in,
    weight_out, public_out, mixture_out, one_out, two_out,
    current, public, mixture, one, two,
    acts, grads, parts, shares, sent, near,
    load_sem, acts_send, acts_recv, grads_send, grads_recv,
    share_send, share_recv, near_send, near_recv, pass_send,
):
    rx, ry, tp = lax.axis_index("rx"), lax.axis_index("ry"), lax.axis_index("tp")
    nrx, nry, ntp = lax.axis_size("rx"), lax.axis_size("ry"), lax.axis_size("tp")
    chip, core = tp // 2, lax.rem(tp, 2)
    other = 1 - core
    row = lax.rem(rx, 4)
    rows, width = weight_in.shape
    tokens = grad_in.shape[0]
    half = width // 2
    step = half // CHUNKS

    def beside(d):
        return (rx, ry, lax.rem(tp + d, ntp))

    def around(drx, dry):
        return (lax.rem(rx + drx + nrx, nrx), lax.rem(ry + dry + nry, nry), tp)

    own_acts = pltpu.make_async_copy(
        stored_in.at[:, pl.ds(pl.multiple_of(chip * 2 * tokens, 128), 2 * tokens)],
        acts.at[tp], load_sem.at[5])
    own_acts.start()
    own_grad = pltpu.make_async_copy(
        grad_in.at[:, pl.ds(pl.multiple_of(core * half, 128), half)],
        grads.at[pl.ds(pl.multiple_of(core * tokens, 128), tokens)], load_sem.at[6])
    own_grad.start()
    loads = []
    for i, (src, dst) in enumerate(
        ((one_in, one), (two_in, two), (weight_in, current), (public_in, public), (mixture_in, mixture))
    ):
        copy = pltpu.make_async_copy(src, dst, load_sem.at[i])
        copy.start()
        loads.append(copy)

    barrier = pltpu.get_barrier_semaphore()

    def greet(who):
        pl.semaphore_signal(barrier, inc=1, device_id=who, device_id_type=MESH)

    pl.when(row == 0)(lambda: greet(around(-2, 0)))
    pl.when(row == 3)(lambda: greet(around(2, 0)))
    for who in (around(1, 0), around(-1, 0), around(0, 1), around(0, -1)):
        greet(who)
    for d in range(1, ntp):
        greet(beside(d))
    passes = (row == 1) | (row == 2)
    pl.semaphore_wait(barrier, ntp - 1 + 4 + jnp.where(passes, 1, 0))

    act_copies = []
    for d in range(1, ntp):
        to = lax.rem(tp + d, ntp)
        act_copies.append(pltpu.make_async_remote_copy(
            src_ref=stored_in.at[:, pl.ds(pl.multiple_of((to // 2) * 2 * tokens, 128), 2 * tokens)],
            dst_ref=acts.at[tp],
            send_sem=acts_send.at[d], recv_sem=acts_recv.at[d],
            device_id=beside(d), device_id_type=MESH))
        act_copies[-1].start()
    grad_copies = []
    for k in range(CHUNKS):
        grad_copies.append(pltpu.make_async_remote_copy(
            src_ref=grad_in.at[:, pl.ds(pl.multiple_of(other * half + k * step, 128), step)],
            dst_ref=grads.at[pl.ds(pl.multiple_of(core * tokens, 128), tokens), pl.ds(k * step, step)],
            send_sem=grads_send.at[k], recv_sem=grads_recv.at[k],
            device_id=(rx, ry, chip * 2 + other), device_id_type=MESH))
        grad_copies[-1].start()

    own_acts.wait()
    own_grad.wait()
    for copy in act_copies:
        copy.wait_recv()
    gathered = acts[...].astype(jnp.float32).reshape(ntp * rows, 2 * tokens).astype(jnp.bfloat16)

    share_copies = []
    for k in range(CHUNKS):
        grad_copies[k].wait_recv()
        terms = jnp.dot(gathered, grads[:, k * step:(k + 1) * step], preferred_element_type=jnp.float32)
        for j in range(ntp):
            parts[k, j] = terms[j * rows:(j + 1) * rows].astype(jnp.bfloat16)
        copies = []
        for d in (4, 3, 5, 2, 6, 7, 1):
            copies.append(pltpu.make_async_remote_copy(
                src_ref=parts.at[k, lax.rem(tp + d, ntp)],
                dst_ref=shares.at[k, tp],
                send_sem=share_send.at[k, d], recv_sem=share_recv.at[k, d],
                device_id=beside(d), device_id_type=MESH))
            copies[-1].start()
        share_copies.append(copies)

    def piece(k, h):
        return slice(None), slice(h * half + k * step, h * half + (k + 1) * step)

    def hop(turn, k, h, slot, who):
        return pltpu.make_async_remote_copy(
            src_ref=sent.at[turn, k, h], dst_ref=near.at[turn, k, h, slot],
            send_sem=near_send.at[turn, k, h, slot], recv_sem=near_recv.at[turn, k, h, slot],
            device_id=who, device_id_type=MESH)

    targets = (around(1, 0), around(-1, 0), around(0, 1), around(0, -1))

    def each_hop(turn, k, h, act):
        for slot in range(4):
            copy = hop(turn, k, h, slot, targets[slot])
            if h == 1 and slot < 2:
                pl.when(row != (3, 0)[slot])(functools.partial(act, copy))
            else:
                act(copy)

    pair = jnp.where(lax.rem(row, 2) == 0, 1, 0)

    def passing(turn, k, up):
        slot = 1 if up else 0
        return pltpu.make_async_remote_copy(
            src_ref=near.at[turn, k, 1, slot], dst_ref=near.at[turn, k, 1, 1 - slot],
            send_sem=pass_send.at[turn, k], recv_sem=near_recv.at[turn, k, 1, 1 - slot],
            device_id=around(2 if up else -2, 0), device_id_type=MESH)

    def arrive(turn, k, h, slot):
        hop(turn, k, h, slot, targets[0]).wait_recv()

    def pass_on(turn, k):
        arrive(turn, k, 1, pair)
        pl.when(row == 2)(lambda: passing(turn, k, True).start())
        pl.when(row == 1)(lambda: passing(turn, k, False).start())

    def start(copy):
        copy.start()

    for copy in loads:
        copy.wait()

    for k in range(CHUNKS):
        for copy in share_copies[k]:
            copy.wait_recv()
        shares[k, tp] = parts[k, tp]
        for h in range(2):
            at = piece(k, h)
            gradient = shares[k, h].astype(jnp.float32)
            for other_chip in range(1, ntp // 2):
                gradient += shares[k, 2 * other_chip + h].astype(jnp.float32)
            first_new = beta_one * one[at] + (1.0 - beta_one) * gradient
            second_new = beta_two * two[at] + (1.0 - beta_two) * gradient * gradient
            one_out[at] = first_new
            two_out[at] = second_new
            adjusted = first_new / first_fix / (jnp.sqrt(second_new / second_fix) + epsilon)
            weight = current[at]
            now = weight - learn_rate * (adjusted + decay_rate * weight)
            current[at] = now
            sent[0, k, h] = (now - public[at]).astype(jnp.bfloat16)
            each_hop(0, k, h, start)
        if k:
            pass_on(0, k - 1)
    pass_on(0, CHUNKS - 1)

    for turn in range(ROUNDS):
        for k in range(CHUNKS):
            for h in range(2):
                at = piece(k, h)
                if h == 0:
                    for slot in range(4):
                        arrive(turn, k, h, slot)
                else:
                    arrive(turn, k, h, 1 - pair)
                    arrive(turn, k, h, 2)
                    arrive(turn, k, h, 3)
                beside_all = near[turn, k, h, 0].astype(jnp.float32)
                for slot in range(1, 4):
                    beside_all += near[turn, k, h, slot].astype(jnp.float32)
                own = sent[turn, k, h].astype(jnp.float32)
                public_new = public[at] + own
                mixture_new = mixture[at] + (own + beside_all) / 5.0
                now = current[at] + step_size * (mixture_new - public_new)
                if turn == ROUNDS - 1:
                    weight_out[at] = now
                    public_out[at] = public_new
                    mixture_out[at] = mixture_new
                else:
                    current[at] = now
                    public[at] = public_new
                    mixture[at] = mixture_new
                    sent[turn + 1, k, h] = (now - public_new).astype(jnp.bfloat16)
                    each_hop(turn + 1, k, h, start)
            if turn < ROUNDS - 1 and k:
                pass_on(turn + 1, k - 1)
        if turn < ROUNDS - 1:
            pass_on(turn + 1, CHUNKS - 1)

    for copy in act_copies + grad_copies:
        copy.wait_send()
    for copies in share_copies:
        for copy in copies:
            copy.wait_send()
    for turn in range(ROUNDS):
        for k in range(CHUNKS):
            for h in range(2):
                each_hop(turn, k, h, lambda copy: copy.wait_send())
            pl.when(passes)(lambda turn=turn, k=k: passing(turn, k, True).wait_send())


def per_device(weight, public, mixture, moment_one, moment_two, stored, out_grad):
    rows, width = weight.shape[2:]
    tokens = out_grad.shape[2]
    step = width // 2 // CHUNKS
    ntp = lax.axis_size("tp")
    whole = jax.ShapeDtypeStruct((rows, width), jnp.float32)
    held = pltpu.VMEM((rows, width), jnp.float32)
    dma = pltpu.SemaphoreType.DMA
    outs = pl.pallas_call(
        kernel,
        out_shape=[whole] * 5,
        in_specs=[pl.BlockSpec(memory_space=pl.ANY)] * 7,
        out_specs=[pl.BlockSpec(memory_space=pltpu.VMEM)] * 5,
        scratch_shapes=[held] * 5 + [
            pltpu.VMEM((ntp, rows, 2 * tokens), jnp.bfloat16),
            pltpu.VMEM((2 * tokens, width // 2), jnp.bfloat16),
            pltpu.VMEM((CHUNKS, ntp, rows, step), jnp.bfloat16),
            pltpu.VMEM((CHUNKS, ntp, rows, step), jnp.bfloat16),
            pltpu.VMEM((ROUNDS, CHUNKS, 2, rows, step), jnp.bfloat16),
            pltpu.VMEM((ROUNDS, CHUNKS, 2, 4, rows, step), jnp.bfloat16),
            dma((7,)), dma((ntp,)), dma((ntp,)), dma((CHUNKS,)), dma((CHUNKS,)),
            dma((CHUNKS, ntp)), dma((CHUNKS, ntp)),
            dma((ROUNDS, CHUNKS, 2, 4)), dma((ROUNDS, CHUNKS, 2, 4)), dma((ROUNDS, CHUNKS)),
        ],
        name="gossip_step",
        compiler_params=pltpu.CompilerParams(collective_id=0, has_side_effects=True),
    )(*(a[0, 0] for a in (weight, public, mixture, moment_one, moment_two, stored, out_grad)))
    return tuple(o[None, None] for o in outs)


def solution(mesh):
    spec = P("rx", "ry", "tp", None)
    return jax.shard_map(
        per_device, mesh=mesh, in_specs=(spec,) * 7, out_specs=(spec,) * 5, check_vma=False
    )
```

time: 131 us -> 74.1 us (0.57)
  Pallas kernels: 0 us -> 66.9 us
  waiting for transfers between devices: 49.5 us -> 0 us
  blocking collectives: 37.7 us -> 0 us
  starting transfers between devices: 37.1 us -> 0 us
  local copies, waits for them, and re-layouts: 2.05 us -> 5.98 us
  other arithmetic: 2.97 us -> 0 us
    pallas_call x0 -> x1, Pallas kernels: none -> 66.9 us  [per_device(): pl.pallas_call(kernel, out_shape=[whole] * 5, in_specs=[pl.BlockSpec(memo...]
    ppermute x8 -> x0, waiting for transfers between devices: 49.5 us -> none  [the longest x4 32.8 us: with_halo(): lax.ppermute(last, axis, up)]
    all_to_all x2 -> x0, blocking collectives: 37.7 us -> none  [the longest x1 23.7 us: sum_at_owner(): lax.all_to_all(cut_along(shard, dim, devices), axis, 0, 0, tiled=True)]
    ppermute x8 -> x0, starting transfers between devices: 37.1 us -> none  [the longest x4 28 us: with_halo(): lax.ppermute(initial, axis, [(b, a) for a, b in up])]
    unnamed x13, local copies, waits for them, and re-layouts: 2.04 us -> 5.98 us
    convert_element_type x2 -> x0, other arithmetic: 1.4 us -> none  [per_device(): sent = (current - public_new).astype(jnp.bfloat16)]
    add x1 -> x0, other arithmetic: 1.36 us -> none  [per_device(): current = current + step_size * (mixture_new - public_new)]
  transfers between devices with their start and end apart: 8 -> 0, of which waited for: 7 -> 0; matrix products, arithmetic and copies ran while one was open for 0% -> 0% of each run, Pallas kernels for 0% -> 0%
where the time goes in v1:
time: 74.1 us; the launch traced here: 73.6 us
  Pallas kernels  66.9 us (90%)
  local copies, waits for them, and re-layouts  5.98 us (8%)
    pallas_call x1, Pallas kernels, per_device(): pl.pallas_call(kernel, out_shape=[whole] * 5, in_specs=[pl.BlockSpec(memo...  66.9 us
    unnamed x13, local copies, waits for them, and re-layouts  5.98 us

profile of v1, /device:TPU:1, one launch (start us, length us, event | category | flops | bytes accessed | tf_op | source)
XLA Modules:
  0.0 73.6 jit_solution(6058763197203288483)
XLA Ops:
  0.6 66.9 %gossip_step.1 = (f32[24,4096]{1,0:T(8,128)}, f32[24,4096]{1,0:T(8,128)}, f32[24,4096]{1,0:T(8,128)}, f32[24,4096]{1,0:T(8,128)}, f32[24,4096]{1,0:T(8,128)}) custom-call(f32[24,4096]{1,0:T(8,128)} %bitcast.13, f32[24,4096]{1,0:T(8,128)} %bitcast.14, f32[24,4096]{1,0:T(8,128)} %bitcast.15, f32[24,4096]{1,0:T(8,128)} %bitcast.16, f32[24,4096]{1,0:T(8,128)} %bitcast.17, ...), custom_call_target="tpu_custom_call" | custom-call | tf_op jit(solution)/shard_map/gossip_step/pallas_call | solution.py:236
  67.6 0.0 copy-start.3
  67.6 1.8 %copy.17 = f32[1,1,24,4096]{3,2,1,0:T(8,128)} copy(f32[1,1,24,4096]{3,2,1,0:T(8,128)} %bitcast.22) | data formatting | bytes 786432
  69.4 0.0 copy-done.3
  69.4 0.0 copy-start.2
  69.4 0.7 %copy.18 = f32[1,1,24,4096]{3,2,1,0:T(8,128)} copy(f32[1,1,24,4096]{3,2,1,0:T(8,128)S(1)} %bitcast.21) | data formatting | bytes 786432
  70.2 0.4 copy-done.2
  70.6 0.0 copy-start.1
  70.6 0.7 %copy.19 = f32[1,1,24,4096]{3,2,1,0:T(8,128)} copy(f32[1,1,24,4096]{3,2,1,0:T(8,128)S(1)} %bitcast.20) | data formatting | bytes 786432
  71.3 0.4 copy-done.1
  71.7 0.0 copy-start
  71.7 0.7 %copy.20 = f32[1,1,24,4096]{3,2,1,0:T(8,128)} copy(f32[1,1,24,4096]{3,2,1,0:T(8,128)S(1)} %bitcast.19) | data formatting | bytes 786432
  72.4 0.4 copy-done
  72.8 0.7 %copy.21 = f32[1,1,24,4096]{3,2,1,0:T(8,128)} copy(f32[1,1,24,4096]{3,2,1,0:T(8,128)S(1)} %bitcast.18) | data formatting | bytes 786432
Async XLA Ops:
  67.6 1.8 %copy-start.3 = (f32[24,4096]{1,0:T(8,128)S(1)}, f32[24,4096]{1,0:T(8,128)}, u32[]{:S(2)}) copy-start(f32[24,4096]{1,0:T(8,128)} %get-tuple-element.11) | copy-start | bytes 1179652
  69.4 1.1 %copy-start.2 = (f32[24,4096]{1,0:T(8,128)S(1)}, f32[24,4096]{1,0:T(8,128)}, u32[]{:S(2)}) copy-start(f32[24,4096]{1,0:T(8,128)} %get-tuple-element.12) | copy-start | bytes 1179652
  70.6 1.1 %copy-start.1 = (f32[24,4096]{1,0:T(8,128)S(1)}, f32[24,4096]{1,0:T(8,128)}, u32[]{:S(2)}) copy-start(f32[24,4096]{1,0:T(8,128)} %get-tuple-element.13) | copy-start | bytes 1179652
  71.7 1.1 %copy-start = (f32[24,4096]{1,0:T(8,128)S(1)}, f32[24,4096]{1,0:T(8,128)}, u32[]{:S(2)}) copy-start(f32[24,4096]{1,0:T(8,128)} %get-tuple-element.14) | copy-start | bytes 1179652

commit v2 on v1

--- a/solution.py
+++ b/solution.py
@@ -10,6 +10,8 @@
 MESH = pl.DeviceIdType.MESH
 ROUNDS = 2
 CHUNKS = 4
+AHEAD = 2
+LAG = 2
 
 beta_one = 0.9
 beta_two = 0.95
@@ -27,7 +29,7 @@
     current, public, mixture, one, two,
     acts, grads, parts, shares, sent, near,
     load_sem, acts_send, acts_recv, grads_send, grads_recv,
-    share_send, share_recv, near_send, near_recv, pass_send,
+    share_send, share_recv, near_send, near_recv, pass_send, turn_send, word,
 ):
     rx, ry, tp = lax.axis_index("rx"), lax.axis_index("ry"), lax.axis_index("tp")
     nrx, nry, ntp = lax.axis_size("rx"), lax.axis_size("ry"), lax.axis_size("tp")
@@ -61,19 +63,29 @@
         copy.start()
         loads.append(copy)
 
+    def along(d):
+        z = lax.rem(rx // 4 * nry + ry + d + 2 * nry, 2 * nry)
+        return (z // nry * 4 + row, lax.rem(z, nry), tp)
+
     barrier = pltpu.get_barrier_semaphore()
-
-    def greet(who):
+    near_by = [beside(d) for d in range(1, ntp)] + [along(1), along(-1)]
+    near_by += [(rx // 4 * 4 + lax.rem(row + d, 4), ry, tp) for d in range(1, 4)]
+    for who in near_by:
         pl.semaphore_signal(barrier, inc=1, device_id=who, device_id_type=MESH)
-
-    pl.when(row == 0)(lambda: greet(around(-2, 0)))
-    pl.when(row == 3)(lambda: greet(around(2, 0)))
-    for who in (around(1, 0), around(-1, 0), around(0, 1), around(0, -1)):
-        greet(who)
-    for d in range(1, ntp):
-        greet(beside(d))
-    passes = (row == 1) | (row == 2)
-    pl.semaphore_wait(barrier, ntp - 1 + 4 + jnp.where(passes, 1, 0))
+    pl.semaphore_wait(barrier, len(near_by))
+
+    spans = (1, 2, 4, 1)
+
+    def tell(i):
+        for who in (along(spans[i]), along(-spans[i])):
+            pl.semaphore_signal(word.at[i], inc=1, device_id=who, device_id_type=MESH)
+
+    def hear(i):
+        pl.semaphore_wait(word.at[i], 2)
+
+    edge = (ry == 0) | (ry == nry - 1)
+    passes = ((row == 1) | (row == 2)) & ~edge
+    corner = ((row == 0) | (row == 3)) & edge
 
     act_copies = []
     for d in range(1, ntp):
@@ -93,10 +105,15 @@
             device_id=(rx, ry, chip * 2 + other), device_id_type=MESH))
         grad_copies[-1].start()
 
+    tell(0)
+    hear(0)
+    tell(1)
     own_acts.wait()
     own_grad.wait()
     for copy in act_copies:
         copy.wait_recv()
+    hear(1)
+    tell(2)
     gathered = acts[...].astype(jnp.float32).reshape(ntp * rows, 2 * tokens).astype(jnp.bfloat16)
 
     share_copies = []
@@ -129,8 +146,9 @@
     def each_hop(turn, k, h, act):
         for slot in range(4):
             copy = hop(turn, k, h, slot, targets[slot])
-            if h == 1 and slot < 2:
-                pl.when(row != (3, 0)[slot])(functools.partial(act, copy))
+            if slot < 2:
+                here = row != (3, 0)[slot]
+                pl.when(here if h else here | ~edge)(functools.partial(act, copy))
             else:
                 act(copy)
 
@@ -148,14 +166,38 @@
 
     def pass_on(turn, k):
         arrive(turn, k, 1, pair)
-        pl.when(row == 2)(lambda: passing(turn, k, True).start())
-        pl.when(row == 1)(lambda: passing(turn, k, False).start())
+        pl.when(passes & (row == 2))(lambda: passing(turn, k, True).start())
+        pl.when(passes & (row == 1))(lambda: passing(turn, k, False).start())
+
+    wrap = jnp.where(ry == 0, 2, 3)
+    beyond = jnp.where(row == 3, 0, 1)
+    over = (lax.rem(rx + jnp.where(row == 3, 1, nrx - 1), nrx), nry - 1 - ry, tp)
+
+    def turning(turn, k, h):
+        return pltpu.make_async_remote_copy(
+            src_ref=near.at[turn, k, h, wrap], dst_ref=near.at[turn, k, h, beyond],
+            send_sem=turn_send.at[turn, k, h], recv_sem=near_recv.at[turn, k, h, beyond],
+            device_id=over, device_id_type=MESH)
+
+    bent = [0] * ROUNDS
+
+    def bend(turn, last):
+        while bent[turn] <= min(last, CHUNKS - 1):
+            k = bent[turn]
+            bent[turn] += 1
+            for h in range(2):
+                @pl.when(corner)
+                def _():
+                    arrive(turn, k, h, wrap)
+                    turning(turn, k, h).start()
 
     def start(copy):
         copy.start()
 
     for copy in loads:
         copy.wait()
+    hear(2)
+    tell(3)
 
     for k in range(CHUNKS):
         for copy in share_copies[k]:
@@ -175,6 +217,8 @@
             now = weight - learn_rate * (adjusted + decay_rate * weight)
             current[at] = now
             sent[0, k, h] = (now - public[at]).astype(jnp.bfloat16)
+            if k == 0 and h == 0:
+                hear(3)
             each_hop(0, k, h, start)
         if k:
             pass_on(0, k - 1)
@@ -182,15 +226,14 @@
 
     for turn in range(ROUNDS):
         for k in range(CHUNKS):
+            bend(turn, k + AHEAD - 1)
             for h in range(2):
                 at = piece(k, h)
+                pl.when(~corner)(functools.partial(arrive, turn, k, h, wrap))
+                arrive(turn, k, h, 5 - wrap)
+                arrive(turn, k, h, 1 - pair)
                 if h == 0:
-                    for slot in range(4):
-                        arrive(turn, k, h, slot)
-                else:
-                    arrive(turn, k, h, 1 - pair)
-                    arrive(turn, k, h, 2)
-                    arrive(turn, k, h, 3)
+                    arrive(turn, k, h, pair)
                 beside_all = near[turn, k, h, 0].astype(jnp.float32)
                 for slot in range(1, 4):
                     beside_all += near[turn, k, h, slot].astype(jnp.float32)
@@ -208,8 +251,11 @@
                     mixture[at] = mixture_new
                     sent[turn + 1, k, h] = (now - public_new).astype(jnp.bfloat16)
                     each_hop(turn + 1, k, h, start)
-            if turn < ROUNDS - 1 and k:
-                pass_on(turn + 1, k - 1)
+            if turn < ROUNDS - 1:
+                if k:
+                    pass_on(turn + 1, k - 1)
+                if k >= LAG:
+                    bend(turn + 1, k - LAG)
         if turn < ROUNDS - 1:
             pass_on(turn + 1, CHUNKS - 1)
 
@@ -222,7 +268,17 @@
         for k in range(CHUNKS):
             for h in range(2):
                 each_hop(turn, k, h, lambda copy: copy.wait_send())
+                pl.when(corner)(lambda turn=turn, k=k, h=h: turning(turn, k, h).wait_send())
             pl.when(passes)(lambda turn=turn, k=k: passing(turn, k, True).wait_send())
+
+
+def store(*refs):
+    srcs, dsts, sems = refs[:5], refs[5:10], refs[10]
+    copies = [pltpu.make_async_copy(src, dst, sems.at[i]) for i, (src, dst) in enumerate(zip(srcs, dsts))]
+    for copy in copies:
+        copy.start()
+    for copy in copies:
+        copy.wait()
 
 
 def per_device(weight, public, mixture, moment_one, moment_two, stored, out_grad):
@@ -235,7 +291,7 @@
     dma = pltpu.SemaphoreType.DMA
     outs = pl.pallas_call(
         kernel,
-        out_shape=[whole] * 5,
+        out_shape=[pltpu.VMEM((rows, width), jnp.float32)] * 5,
         in_specs=[pl.BlockSpec(memory_space=pl.ANY)] * 7,
         out_specs=[pl.BlockSpec(memory_space=pltpu.VMEM)] * 5,
         scratch_shapes=[held] * 5 + [
@@ -247,11 +303,20 @@
             pltpu.VMEM((ROUNDS, CHUNKS, 2, 4, rows, step), jnp.bfloat16),
             dma((7,)), dma((ntp,)), dma((ntp,)), dma((CHUNKS,)), dma((CHUNKS,)),
             dma((CHUNKS, ntp)), dma((CHUNKS, ntp)),
-            dma((ROUNDS, CHUNKS, 2, 4)), dma((ROUNDS, CHUNKS, 2, 4)), dma((ROUNDS, CHUNKS)),
+            dma((ROUNDS, CHUNKS, 2, 4)), dma((ROUNDS, CHUNKS, 2, 4)), dma((ROUNDS, CHUNKS)), dma((ROUNDS, CHUNKS, 2)),
+            pltpu.SemaphoreType.REGULAR((4,)),
         ],
         name="gossip_step",
         compiler_params=pltpu.CompilerParams(collective_id=0, has_side_effects=True),
     )(*(a[0, 0] for a in (weight, public, mixture, moment_one, moment_two, stored, out_grad)))
+    outs = pl.pallas_call(
+        store,
+        out_shape=[whole] * 5,
+        in_specs=[pl.BlockSpec(memory_space=pltpu.VMEM)] * 5,
+        out_specs=[pl.BlockSpec(memory_space=pl.ANY)] * 5,
+        scratch_shapes=[dma((5,))],
+        name="store",
+    )(*(pltpu.with_memory_space_constraint(o, pltpu.VMEM) for o in outs))
     return tuple(o[None, None] for o in outs)
 
 

time: 74.1 us -> 66 us (0.89)
  local copies, waits for them, and re-layouts: 5.98 us -> 0 us
  Pallas kernels: 66.9 us -> 65.2 us
    unnamed x13 -> x0, local copies, waits for them, and re-layouts: 5.98 us -> none
    pallas_call x1 -> x2, Pallas kernels: 66.9 us -> 65.2 us  [the longest x1 63.9 us: per_device(): pl.pallas_call(kernel, out_shape=[pltpu.VMEM((rows, width), jnp.float32)]...]
where the time goes in v2:
time: 66 us; the launch traced here: 65.9 us
  Pallas kernels  65.2 us (99%)
    pallas_call x1, Pallas kernels, per_device(): pl.pallas_call(kernel, out_shape=[pltpu.VMEM((rows, width), jnp.float32)]...  63.9 us

profile of v2, /device:TPU:1, one launch (start us, length us, event | category | flops | bytes accessed | tf_op | source)
XLA Modules:
  0.0 65.9 jit_solution(918433458702608089)
XLA Ops:
  0.6 63.9 %gossip_step.1 = (f32[24,4096]{1,0:T(8,128)S(1)}, f32[24,4096]{1,0:T(8,128)S(1)}, f32[24,4096]{1,0:T(8,128)S(1)}, f32[24,4096]{1,0:T(8,128)S(1)}, f32[24,4096]{1,0:T(8,128)S(1)}) custom-call(f32[24,4096]{1,0:T(8,128)} %bitcast.13, f32[24,4096]{1,0:T(8,128)} %bitcast.14, f32[24,4096]{1,0:T(8,128)} %bitcast.15, f32[24,4096]{1,0:T(8,128)} %bitcast.16, ...), custom_call_target="tpu_custom_call" | custom-call | tf_op jit(solution)/shard_map/gossip_step/pallas_call | solution.py:292
  64.6 1.3 %store.1 = (f32[24,4096]{1,0:T(8,128)}, f32[24,4096]{1,0:T(8,128)}, f32[24,4096]{1,0:T(8,128)}, f32[24,4096]{1,0:T(8,128)}, f32[24,4096]{1,0:T(8,128)}) custom-call(f32[24,4096]{1,0:T(8,128)S(1)} %get-tuple-element.15.refs_0_, f32[24,4096]{1,0:T(8,128)S(1)} %get-tuple-element.16.refs_1_, f32[24,4096]{1,0:T(8,128)S(1)} %get-tuple-element.17.refs_2_, ...), custom_call_target="tpu_custom_call" | custom-call | tf_op jit(solution)/shard_map/store/pallas_call | solution.py:312

commit v3 on v2

--- a/solution.py
+++ b/solution.py
@@ -9,8 +9,10 @@
 
 MESH = pl.DeviceIdType.MESH
 ROUNDS = 2
-CHUNKS = 4
-AHEAD = 2
+WIDTHS = (256, 512, 640, 640)
+CHUNKS = len(WIDTHS)
+LATE = (0, 2)
+AHEAD = ((2, 2), (2, 4))
 LAG = 2
 
 beta_one = 0.9
@@ -39,7 +41,10 @@
     rows, width = weight_in.shape
     tokens = grad_in.shape[0]
     half = width // 2
-    step = half // CHUNKS
+    begin = [sum(WIDTHS[:k]) for k in range(CHUNKS)]
+
+    def cut(k):
+        return slice(None), pl.ds(0, WIDTHS[k])
 
     def beside(d):
         return (rx, ry, lax.rem(tp + d, ntp))
@@ -55,14 +60,6 @@
         grad_in.at[:, pl.ds(pl.multiple_of(core * half, 128), half)],
         grads.at[pl.ds(pl.multiple_of(core * tokens, 128), tokens)], load_sem.at[6])
     own_grad.start()
-    loads = []
-    for i, (src, dst) in enumerate(
-        ((one_in, one), (two_in, two), (weight_in, current), (public_in, public), (mixture_in, mixture))
-    ):
-        copy = pltpu.make_async_copy(src, dst, load_sem.at[i])
-        copy.start()
-        loads.append(copy)
-
     def along(d):
         z = lax.rem(rx // 4 * nry + ry + d + 2 * nry, 2 * nry)
         return (z // nry * 4 + row, lax.rem(z, nry), tp)
@@ -99,13 +96,21 @@
     grad_copies = []
     for k in range(CHUNKS):
         grad_copies.append(pltpu.make_async_remote_copy(
-            src_ref=grad_in.at[:, pl.ds(pl.multiple_of(other * half + k * step, 128), step)],
-            dst_ref=grads.at[pl.ds(pl.multiple_of(core * tokens, 128), tokens), pl.ds(k * step, step)],
+            src_ref=grad_in.at[:, pl.ds(pl.multiple_of(other * half + begin[k], 128), WIDTHS[k])],
+            dst_ref=grads.at[pl.ds(pl.multiple_of(core * tokens, 128), tokens), pl.ds(begin[k], WIDTHS[k])],
             send_sem=grads_send.at[k], recv_sem=grads_recv.at[k],
             device_id=(rx, ry, chip * 2 + other), device_id_type=MESH))
         grad_copies[-1].start()
 
     tell(0)
+    loads = []
+    for i, (src, dst) in enumerate(
+        ((one_in, one), (two_in, two), (weight_in, current), (public_in, public), (mixture_in, mixture))
+    ):
+        copy = pltpu.make_async_copy(src, dst, load_sem.at[i])
+        copy.start()
+        loads.append(copy)
+
     hear(0)
     tell(1)
     own_acts.wait()
@@ -119,45 +124,60 @@
     share_copies = []
     for k in range(CHUNKS):
         grad_copies[k].wait_recv()
-        terms = jnp.dot(gathered, grads[:, k * step:(k + 1) * step], preferred_element_type=jnp.float32)
+        terms = jnp.dot(gathered, grads[:, begin[k]:begin[k] + WIDTHS[k]], preferred_element_type=jnp.float32)
         for j in range(ntp):
-            parts[k, j] = terms[j * rows:(j + 1) * rows].astype(jnp.bfloat16)
+            parts[(k, j) + cut(k)] = terms[j * rows:(j + 1) * rows].astype(jnp.bfloat16)
         copies = []
         for d in (4, 3, 5, 2, 6, 7, 1):
             copies.append(pltpu.make_async_remote_copy(
-                src_ref=parts.at[k, lax.rem(tp + d, ntp)],
-                dst_ref=shares.at[k, tp],
+                src_ref=parts.at[(k, lax.rem(tp + d, ntp)) + cut(k)],
+                dst_ref=shares.at[(k, tp) + cut(k)],
                 send_sem=share_send.at[k, d], recv_sem=share_recv.at[k, d],
                 device_id=beside(d), device_id_type=MESH))
             copies[-1].start()
         share_copies.append(copies)
 
     def piece(k, h):
-        return slice(None), slice(h * half + k * step, h * half + (k + 1) * step)
+        return slice(None), slice(h * half + begin[k], h * half + begin[k] + WIDTHS[k])
 
     def hop(turn, k, h, slot, who):
         return pltpu.make_async_remote_copy(
-            src_ref=sent.at[turn, k, h], dst_ref=near.at[turn, k, h, slot],
+            src_ref=sent.at[(turn, k, h) + cut(k)], dst_ref=near.at[(turn, k, h, slot) + cut(k)],
             send_sem=near_send.at[turn, k, h, slot], recv_sem=near_recv.at[turn, k, h, slot],
             device_id=who, device_id_type=MESH)
 
     targets = (around(1, 0), around(-1, 0), around(0, 1), around(0, -1))
+
+    early = rx < nrx // 2
+
+    def each_far(turn, k, act):
+        for slot in range(2):
+            copy = hop(turn, k, 0, slot, targets[slot])
+            pl.when(early & (row == (3, 0)[slot]) & ~edge)(functools.partial(act, copy))
 
     def each_hop(turn, k, h, act):
         for slot in range(4):
             copy = hop(turn, k, h, slot, targets[slot])
             if slot < 2:
                 here = row != (3, 0)[slot]
-                pl.when(here if h else here | ~edge)(functools.partial(act, copy))
+                far = ~edge & ~early if turn else ~edge
+                pl.when(here if h else here | far)(functools.partial(act, copy))
             else:
-                act(copy)
+                pl.when(ry == (nry - 1, 0)[slot - 2])(functools.partial(act, copy))
+
+    def each_step(turn, k, act, some=None):
+        for h in range(2):
+            for slot in range(2, 4):
+                copy = hop(turn, k, h, slot, targets[slot])
+                here = ry != (nry - 1, 0)[slot - 2]
+                pl.when(here if some is None else here & some)(functools.partial(act, copy))
 
     pair = jnp.where(lax.rem(row, 2) == 0, 1, 0)
 
     def passing(turn, k, up):
         slot = 1 if up else 0
         return pltpu.make_async_remote_copy(
-            src_ref=near.at[turn, k, 1, slot], dst_ref=near.at[turn, k, 1, 1 - slot],
+            src_ref=near.at[(turn, k, 1, slot) + cut(k)], dst_ref=near.at[(turn, k, 1, 1 - slot) + cut(k)],
             send_sem=pass_send.at[turn, k], recv_sem=near_recv.at[turn, k, 1, 1 - slot],
             device_id=around(2 if up else -2, 0), device_id_type=MESH)
 
@@ -166,8 +186,13 @@
 
     def pass_on(turn, k):
         arrive(turn, k, 1, pair)
-        pl.when(passes & (row == 2))(lambda: passing(turn, k, True).start())
-        pl.when(passes & (row == 1))(lambda: passing(turn, k, False).start())
+        now = ~early if turn else True
+        pl.when(passes & (row == 2) & now)(lambda: passing(turn, k, True).start())
+        pl.when(passes & (row == 1) & now)(lambda: passing(turn, k, False).start())
+
+    def pass_late(turn, k):
+        pl.when(passes & (row == 2) & early)(lambda: passing(turn, k, True).start())
+        pl.when(passes & (row == 1) & early)(lambda: passing(turn, k, False).start())
 
     wrap = jnp.where(ry == 0, 2, 3)
     beyond = jnp.where(row == 3, 0, 1)
@@ -175,18 +200,19 @@
 
     def turning(turn, k, h):
         return pltpu.make_async_remote_copy(
-            src_ref=near.at[turn, k, h, wrap], dst_ref=near.at[turn, k, h, beyond],
+            src_ref=near.at[(turn, k, h, wrap) + cut(k)], dst_ref=near.at[(turn, k, h, beyond) + cut(k)],
             send_sem=turn_send.at[turn, k, h], recv_sem=near_recv.at[turn, k, h, beyond],
             device_id=over, device_id_type=MESH)
 
-    bent = [0] * ROUNDS
-
-    def bend(turn, last):
-        while bent[turn] <= min(last, CHUNKS - 1):
-            k = bent[turn]
-            bent[turn] += 1
+    bent = {}
+
+    def bend(turn, last, who):
+        here = corner & early if who else corner & ~early
+        while bent.setdefault((turn, who), 0) <= min(last, CHUNKS - 1):
+            k = bent[turn, who]
+            bent[turn, who] += 1
             for h in range(2):
-                @pl.when(corner)
+                @pl.when(here)
                 def _():
                     arrive(turn, k, h, wrap)
                     turning(turn, k, h).start()
@@ -194,20 +220,20 @@
     def start(copy):
         copy.start()
 
+    hear(2)
+    tell(3)
     for copy in loads:
         copy.wait()
-    hear(2)
-    tell(3)
 
     for k in range(CHUNKS):
         for copy in share_copies[k]:
             copy.wait_recv()
-        shares[k, tp] = parts[k, tp]
+        shares[(k, tp) + cut(k)] = parts[(k, tp) + cut(k)]
         for h in range(2):
             at = piece(k, h)
-            gradient = shares[k, h].astype(jnp.float32)
+            gradient = shares[(k, h) + cut(k)].astype(jnp.float32)
             for other_chip in range(1, ntp // 2):
-                gradient += shares[k, 2 * other_chip + h].astype(jnp.float32)
+                gradient += shares[(k, 2 * other_chip + h) + cut(k)].astype(jnp.float32)
             first_new = beta_one * one[at] + (1.0 - beta_one) * gradient
             second_new = beta_two * two[at] + (1.0 - beta_two) * gradient * gradient
             one_out[at] = first_new
@@ -216,17 +242,22 @@
             weight = current[at]
             now = weight - learn_rate * (adjusted + decay_rate * weight)
             current[at] = now
-            sent[0, k, h] = (now - public[at]).astype(jnp.bfloat16)
+            sent[(0, k, h) + cut(k)] = (now - public[at]).astype(jnp.bfloat16)
             if k == 0 and h == 0:
                 hear(3)
             each_hop(0, k, h, start)
         if k:
             pass_on(0, k - 1)
+        if k >= LATE[0]:
+            each_step(0, k - LATE[0], start)
+    for k in range(CHUNKS - LATE[0], CHUNKS):
+        each_step(0, k, start)
     pass_on(0, CHUNKS - 1)
 
     for turn in range(ROUNDS):
         for k in range(CHUNKS):
-            bend(turn, k + AHEAD - 1)
+            bend(turn, k + AHEAD[turn][0] - 1, True)
+            bend(turn, k + AHEAD[turn][1] - 1, False)
             for h in range(2):
                 at = piece(k, h)
                 pl.when(~corner)(functools.partial(arrive, turn, k, h, wrap))
@@ -234,10 +265,10 @@
                 arrive(turn, k, h, 1 - pair)
                 if h == 0:
                     arrive(turn, k, h, pair)
-                beside_all = near[turn, k, h, 0].astype(jnp.float32)
+                beside_all = near[(turn, k, h, 0) + cut(k)].astype(jnp.float32)
                 for slot in range(1, 4):
-                    beside_all += near[turn, k, h, slot].astype(jnp.float32)
-                own = sent[turn, k, h].astype(jnp.float32)
+                    beside_all += near[(turn, k, h, slot) + cut(k)].astype(jnp.float32)
+                own = sent[(turn, k, h) + cut(k)].astype(jnp.float32)
                 public_new = public[at] + own
                 mixture_new = mixture[at] + (own + beside_all) / 5.0
                 now = current[at] + step_size * (mixture_new - public_new)
@@ -249,15 +280,21 @@
                     current[at] = now
                     public[at] = public_new
                     mixture[at] = mixture_new
-                    sent[turn + 1, k, h] = (now - public_new).astype(jnp.bfloat16)
+                    sent[(turn + 1, k, h) + cut(k)] = (now - public_new).astype(jnp.bfloat16)
                     each_hop(turn + 1, k, h, start)
             if turn < ROUNDS - 1:
                 if k:
                     pass_on(turn + 1, k - 1)
                 if k >= LAG:
-                    bend(turn + 1, k - LAG)
+                    bend(turn + 1, k - LAG, True)
+                    bend(turn + 1, k - LAG, False)
+                each_step(turn + 1, k, start, early)
         if turn < ROUNDS - 1:
             pass_on(turn + 1, CHUNKS - 1)
+            for k in range(CHUNKS):
+                each_step(turn + 1, k, start, ~early)
+                each_far(turn + 1, k, start)
+                pass_late(turn + 1, k)
 
     for copy in act_copies + grad_copies:
         copy.wait_send()
@@ -266,6 +303,9 @@
             copy.wait_send()
     for turn in range(ROUNDS):
         for k in range(CHUNKS):
+            each_step(turn, k, lambda copy: copy.wait_send())
+            if turn:
+                each_far(turn, k, lambda copy: copy.wait_send())
             for h in range(2):
                 each_hop(turn, k, h, lambda copy: copy.wait_send())
                 pl.when(corner)(lambda turn=turn, k=k, h=h: turning(turn, k, h).wait_send())
@@ -284,7 +324,8 @@
 def per_device(weight, public, mixture, moment_one, moment_two, stored, out_grad):
     rows, width = weight.shape[2:]
     tokens = out_grad.shape[2]
-    step = width // 2 // CHUNKS
+    step = max(WIDTHS)
+    assert 2 * sum(WIDTHS) == width
     ntp = lax.axis_size("tp")
     whole = jax.ShapeDtypeStruct((rows, width), jnp.float32)
     held = pltpu.VMEM((rows, width), jnp.float32)

time: 66 us -> 62.2 us (0.942)
  the two profiles are of different devices: /device:TPU:1 before, /device:TPU:288 now
where the time goes in v3:
time: 62.2 us; the launch traced here: 62.1 us
  Pallas kernels  61.4 us (99%)
  between operations  0.64 us (1%)
    pallas_call x1, Pallas kernels, per_device(): pl.pallas_call(kernel, out_shape=[pltpu.VMEM((rows, width), jnp.float32)]...  60.1 us
    pallas_call x1, Pallas kernels, per_device(): pl.pallas_call(store, out_shape=[whole] * 5, in_specs=[pl.BlockSpec(memor...  1.31 us

profile of v3, /device:TPU:288, one launch (start us, length us, event | category | flops | bytes accessed | tf_op | source)
XLA Modules:
  0.0 62.1 jit_solution(6507989734518647310)
XLA Ops:
  0.6 60.1 %gossip_step.1 = (f32[24,4096]{1,0:T(8,128)S(1)}, f32[24,4096]{1,0:T(8,128)S(1)}, f32[24,4096]{1,0:T(8,128)S(1)}, f32[24,4096]{1,0:T(8,128)S(1)}, f32[24,4096]{1,0:T(8,128)S(1)}) custom-call(f32[24,4096]{1,0:T(8,128)} %bitcast.13, f32[24,4096]{1,0:T(8,128)} %bitcast.14, f32[24,4096]{1,0:T(8,128)} %bitcast.15, f32[24,4096]{1,0:T(8,128)} %bitcast.16, ...), custom_call_target="tpu_custom_call" | custom-call | tf_op jit(solution)/shard_map/gossip_step/pallas_call | solution.py:333
  60.7 1.3 %store.1 = (f32[24,4096]{1,0:T(8,128)}, f32[24,4096]{1,0:T(8,128)}, f32[24,4096]{1,0:T(8,128)}, f32[24,4096]{1,0:T(8,128)}, f32[24,4096]{1,0:T(8,128)}) custom-call(f32[24,4096]{1,0:T(8,128)S(1)} %get-tuple-element.15.refs_0_, f32[24,4096]{1,0:T(8,128)S(1)} %get-tuple-element.16.refs_1_, f32[24,4096]{1,0:T(8,128)S(1)} %get-tuple-element.17.refs_2_, ...), custom_call_target="tpu_custom_call" | custom-call | tf_op jit(solution)/shard_map/store/pallas_call | solution.py:353

commit v4 on v3

--- a/solution.py
+++ b/solution.py
@@ -11,7 +11,6 @@
 ROUNDS = 2
 WIDTHS = (256, 512, 640, 640)
 CHUNKS = len(WIDTHS)
-LATE = (0, 2)
 AHEAD = ((2, 2), (2, 4))
 LAG = 2
 
@@ -243,15 +242,15 @@
             now = weight - learn_rate * (adjusted + decay_rate * weight)
             current[at] = now
             sent[(0, k, h) + cut(k)] = (now - public[at]).astype(jnp.bfloat16)
-            if k == 0 and h == 0:
-                hear(3)
-            each_hop(0, k, h, start)
+            if k:
+                each_hop(0, k, h, start)
+        each_step(0, k, start)
         if k:
             pass_on(0, k - 1)
-        if k >= LATE[0]:
-            each_step(0, k - LATE[0], start)
-    for k in range(CHUNKS - LATE[0], CHUNKS):
-        each_step(0, k, start)
+        else:
+            hear(3)
+            for h in range(2):
+                each_hop(0, k, h, start)
     pass_on(0, CHUNKS - 1)
 
     for turn in range(ROUNDS):

time: 62.2 us -> 63.2 us (1.016)
  the two profiles are of different devices: /device:TPU:288 before, /device:TPU:32 now
where the time goes in v4:
time: 63.2 us; the launch traced here: 63.1 us
  Pallas kernels  62.5 us (99%)
  between operations  0.64 us (1%)
    pallas_call x1, Pallas kernels, per_device(): pl.pallas_call(kernel, out_shape=[pltpu.VMEM((rows, width), jnp.float32)]...  61.2 us
    pallas_call x1, Pallas kernels, per_device(): pl.pallas_call(store, out_shape=[whole] * 5, in_specs=[pl.BlockSpec(memor...  1.31 us

profile of v4, /device:TPU:32, one launch (start us, length us, event | category | flops | bytes accessed | tf_op | source)
XLA Modules:
  0.0 63.1 jit_solution(16978057268678443820)
XLA Ops:
  0.6 61.2 %gossip_step.1 = (f32[24,4096]{1,0:T(8,128)S(1)}, f32[24,4096]{1,0:T(8,128)S(1)}, f32[24,4096]{1,0:T(8,128)S(1)}, f32[24,4096]{1,0:T(8,128)S(1)}, f32[24,4096]{1,0:T(8,128)S(1)}) custom-call(f32[24,4096]{1,0:T(8,128)} %bitcast.13, f32[24,4096]{1,0:T(8,128)} %bitcast.14, f32[24,4096]{1,0:T(8,128)} %bitcast.15, f32[24,4096]{1,0:T(8,128)} %bitcast.16, ...), custom_call_target="tpu_custom_call" | custom-call | tf_op jit(solution)/shard_map/gossip_step/pallas_call | solution.py:332
  61.8 1.3 %store.1 = (f32[24,4096]{1,0:T(8,128)}, f32[24,4096]{1,0:T(8,128)}, f32[24,4096]{1,0:T(8,128)}, f32[24,4096]{1,0:T(8,128)}, f32[24,4096]{1,0:T(8,128)}) custom-call(f32[24,4096]{1,0:T(8,128)S(1)} %get-tuple-element.15.refs_0_, f32[24,4096]{1,0:T(8,128)S(1)} %get-tuple-element.16.refs_1_, f32[24,4096]{1,0:T(8,128)S(1)} %get-tuple-element.17.refs_2_, ...), custom_call_target="tpu_custom_call" | custom-call | tf_op jit(solution)/shard_map/store/pallas_call | solution.py:352
